TPU v7x, 512 devices: a whole 4x4x16 slice. The times are simulated.
512 devices in a mesh: seq: 64 (over z, x), head: 8 (over y, core).
Axes of the slice: x: 4, y: 4, z: 16, core: 2. Of those that a mesh axis runs over, the one named last changes fastest.
Arguments:
- tokens: bfloat16 [8192, 4096], P('seq', 'head')
- gain: float32 [4096], replicated, may hold values from 0.25 to 1.75
- w_query: bfloat16 [4096, 2048], P('seq', 'head'), may hold values from -0.09375 to 0.09375
- w_key: bfloat16 [4096, 2048], P('seq', 'head'), may hold values from -0.09375 to 0.09375
- w_value: bfloat16 [4096, 2048], P('seq', 'head'), may hold values from -0.09375 to 0.09375
- w_out: bfloat16 [2048, 4096], P('head', 'seq'), may hold values from -0.125 to 0.125
- mem_query: bfloat16 [128, 2048], P(None, 'head'), may hold values from -12 to 12
- score_scale: float32 [16], P('head'), may hold values from 1.5 to 4
- decay: float32 [64, 16], P('seq', 'head'), may hold values from 0 to 1, as said below
- seg_len: int32 [64], P('seq'), may hold values from 32 to 128, as said below
Outputs:
- branch: bfloat16 [8192, 4096], P('seq', 'head')
Inputs may be any that keep to these rules, and one draw needn't show every extreme that they name: `decay`: retention lies strictly between 0 and 1. `seg_len`: at least one segment is full and at least one holds exactly 32 valid tokens.
All inputs are finite; a program needn't handle non-finite values.
Results may differ from a plain program's by a relative error of at most 0.015.
Values may be sent and summed in bfloat16 or wider, within the bound.
A program may use at most 64 MiB of HBM per device.

v0:
```python
import math
import jax
import jax.numpy as jnp
from jax import lax
from jax.sharding import PartitionSpec as P

DH = 128


def carried_in(part, axis, combine, identity):
    place = lax.axis_index(axis)
    gathered = jax.tree.map(lambda a: lax.all_gather(a, axis), part)
    state = jax.tree.map(lambda a, e: jnp.zeros_like(a) + jnp.asarray(e, a.dtype), part, identity)

    def one(lap, state):
        return combine(
            state, jax.tree.map(lambda a: lax.dynamic_index_in_dim(a, lap, 0, False), gathered)
        )

    return lax.fori_loop(0, place, one, state)


def body(tokens, gain, w_query, w_key, w_value, w_out, mem_query, score_scale, decay, seg_len):
    seg_rows, feat_local = tokens.shape
    col_local = w_query.shape[1]
    head_size = DH
    heads_local = col_local // head_size
    slot_count = mem_query.shape[0]
    valid_len = seg_len[0]
    inverse_root_scale = 1.0 / math.sqrt(head_size)
    score_bias = math.log(slot_count + seg_rows)
    whole = lax.all_gather(tokens, "head", axis=1, tiled=True)
    wide = whole.astype(jnp.float32)
    mean_squares = jnp.mean(wide * wide, axis=1, keepdims=True)
    normed = (wide * lax.rsqrt(mean_squares + 1e-05) * gain).astype(jnp.bfloat16)
    pieces = (
        lax.all_gather(w_query, "seq", axis=0, tiled=True),
        lax.all_gather(w_key, "seq", axis=0, tiled=True),
        lax.all_gather(w_value, "seq", axis=0, tiled=True),
    )
    query_sum, key_sum, value_sum = tuple(
        (jnp.dot(normed, piece, preferred_element_type=jnp.float32) for piece in pieces)
    )
    query_head_split = query_sum.astype(jnp.bfloat16).reshape(seg_rows, heads_local, head_size)
    key_head_split = key_sum.astype(jnp.bfloat16).reshape(seg_rows, heads_local, head_size)
    value_head_split = value_sum.astype(jnp.bfloat16).reshape(seg_rows, heads_local, head_size)
    positions = jnp.arange(seg_rows, dtype=jnp.int32)
    valid_keys = (positions < valid_len).astype(jnp.float32)
    memory_head_split = mem_query.reshape(slot_count, heads_local, head_size)
    memory_write_scores = (
        jnp.einsum(
            "bia,sia->ibs", memory_head_split, key_head_split, preferred_element_type=jnp.float32
        )
        * inverse_root_scale
    )
    memory_write_weights = (
        jax.nn.sigmoid(memory_write_scores - math.log(seg_rows)) * valid_keys[None, None, :]
    ).astype(jnp.bfloat16)
    memory_written_keys = jnp.einsum(
        "elz,zek->lek", memory_write_weights, key_head_split, preferred_element_type=jnp.float32
    )
    memory_written_values = jnp.einsum(
        "elz,zek->lek", memory_write_weights, value_head_split, preferred_element_type=jnp.float32
    )
    written = jnp.stack(
        [
            memory_written_keys.reshape(slot_count, col_local),
            memory_written_values.reshape(slot_count, col_local),
        ]
    )

    def combine_state(earlier, later):
        return (
            earlier[0] * later[0],
            jnp.repeat(later[0], head_size)[None, None, :] * earlier[1] + later[1],
        )

    retain = decay[0]
    identity = (jnp.ones_like(retain), jnp.zeros_like(written))
    _, memory_in = carried_in((retain, written), "seq", combine_state, identity)
    mem_split = memory_in.reshape(2, slot_count, heads_local, head_size)
    memory_unit_rows = (
        mem_split * lax.rsqrt(jnp.mean(jnp.square(mem_split), axis=3, keepdims=True) + 1e-06)
    ).astype(jnp.bfloat16)
    head_scale_factors = (score_scale * inverse_root_scale)[:, None, None]
    memory_score_matrix = (
        jnp.einsum(
            "zul,rul->uzr",
            query_head_split,
            memory_unit_rows[0],
            preferred_element_type=jnp.float32,
        )
        * head_scale_factors
    )
    tok_scores = (
        jnp.einsum(
            "thd,shd->hts", query_head_split, key_head_split, preferred_element_type=jnp.float32
        )
        * head_scale_factors
    )
    allowed = (positions[None, :] <= positions[:, None]).astype(jnp.float32) * valid_keys[None, :]
    memory_attention_weights = jax.nn.sigmoid(memory_score_matrix - score_bias).astype(jnp.bfloat16)
    token_attention_weights = (
        jax.nn.sigmoid(tok_scores - score_bias) * allowed[None, :, :]
    ).astype(jnp.bfloat16)
    attended_output = jnp.einsum(
        "krf,fku->rku",
        memory_attention_weights,
        memory_unit_rows[1],
        preferred_element_type=jnp.float32,
    )
    attended_output = attended_output + jnp.einsum(
        "ymo,oyl->myl",
        token_attention_weights,
        value_head_split,
        preferred_element_type=jnp.float32,
    )
    attended_output = (
        (attended_output * valid_keys[:, None, None])
        .astype(jnp.bfloat16)
        .reshape(seg_rows, col_local)
    )
    partial_rows = jnp.dot(
        attended_output,
        lax.all_gather(w_out, "seq", axis=1, tiled=True),
        preferred_element_type=jnp.float32,
    )
    branch = lax.psum_scatter(
        partial_rows.astype(jnp.bfloat16), "head", scatter_dimension=1, tiled=True
    )
    return branch


def solution(mesh):
    return jax.shard_map(
        body,
        mesh=mesh,
        in_specs=(
            P("seq", "head"),
            P(),
            P("seq", "head"),
            P("seq", "head"),
            P("seq", "head"),
            P("head", "seq"),
            P(None, "head"),
            P("head"),
            P("seq", "head"),
            P("seq"),
        ),
        out_specs=P("seq", "head"),
        check_vma=False,
    )
```

profile of v0, /device:TPU:2, one launch (start us, length us, event | category | flops | bytes accessed | tf_op | source)
XLA Modules:
  0.0 846.3 jit_solution(12068725102322100497)
XLA Ops:
  6.5 0.0 copy-start
  6.5 0.0 all-gather.9.cloned.1.call-start
  6.5 0.7 all-gather.9.cloned.1.call-update
  7.3 0.0 all-gather.11.cloned.1.call-start
  7.3 0.7 all-gather.11.cloned.1.call-update
  8.0 0.0 all-gather.13.cloned.1.call-start
  8.1 0.7 all-gather.13.cloned.1.call-update
  8.7 0.0 all-gather.15.cloned.1.call-start
  8.8 0.5 all-gather.15.cloned.1.call-update
  9.3 0.0 all-gather.19.cloned.1.call-start
  10.0 34.9 %all-gather.9.cloned.1.call-done = bf16[128,4096]{1,0:T(8,128)(2,1)} async-done(((bf16[128,512]{1,0:T(8,128)(2,1)}), bf16[128,4096]{1,0:T(8,128)(2,1)}) %all-gather.9.cloned.1.call-update) | async-done | bytes 1048592 | tf_op jit(solution)/shard_map/all_gather | solution.py:32
  44.9 1.5 fusion
  46.4 0.0 copy-start.3
  46.4 141.3 %all-gather.11.cloned.1.call-done = bf16[4096,256]{1,0:T(8,128)(2,1)} async-done(((bf16[64,256]{1,0:T(8,128)(2,1)}), bf16[4096,256]{1,0:T(8,128)(2,1)}) %all-gather.11.cloned.1.call-update) | async-done | bytes 2097168 | tf_op jit(solution)/shard_map/all_gather | solution.py:38
  187.8 2.4 convolution_convert_fusion.3
  190.2 0.1 copy.33
  190.3 0.0 copy-done
  190.3 0.2 fusion.24
  190.6 0.1 fusion.52
  190.7 0.1 copy.25
  190.9 0.0 copy-start.2
  190.9 0.0 copy-start.4
  190.9 136.7 %all-gather.13.cloned.1.call-done = bf16[4096,256]{1,0:T(8,128)(2,1)} async-done(((bf16[64,256]{1,0:T(8,128)(2,1)}), bf16[4096,256]{1,0:T(8,128)(2,1)}) %all-gather.13.cloned.1.call-update) | async-done | bytes 2097168 | tf_op jit(solution)/shard_map/all_gather | solution.py:39
  327.6 0.0 copy-done.1
  327.6 0.0 copy-done.3
  327.6 2.1 convolution_convert_fusion.2
  329.7 0.1 copy.32
  329.9 0.2 fusion.53
  330.0 0.1 copy.26
  330.1 0.7 pad_maximum_fusion
  330.8 0.0 all-gather.19.cloned.1.call-update
  330.9 0.0 all-gather.17.cloned.1.call-start
  330.9 0.5 all-gather.17.cloned.1.call-update
  331.5 0.0 reduce-scatter.2.cloned.1.call-start
  331.5 72.5 %all-gather.1 = f32[64,1,2]{2,1,0:T(1,128)S(1)} all-gather(f32[1,1,2]{2,1,0:T(1,128)S(1)} %bitcast.76), channel_id=1, replica_groups=mesh['seq'=64,'head'=8] {'seq'}, dimensions={0}, use_global_device_ids=true | all-gather | bytes 520 | tf_op jit(solution)/shard_map/all_gather | solution.py:12
  404.0 63.3 %all-gather.15.cloned.1.call-done = bf16[4096,256]{1,0:T(8,128)(2,1)} async-done(((bf16[64,256]{1,0:T(8,128)(2,1)}), bf16[4096,256]{1,0:T(8,128)(2,1)}) %all-gather.15.cloned.1.call-update) | async-done | bytes 2097168 | tf_op jit(solution)/shard_map/all_gather | solution.py:37
  467.3 2.1 fusion.26
  469.4 189.2 %all-gather.19.cloned.1.call-done = f32[128,128,256]{2,1,0:T(8,128)} async-done(((f32[2,128,256]{2,1,0:T(8,128)}), f32[128,128,256]{2,1,0:T(8,128)}) %all-gather.19.cloned.1.call-update) | async-done | bytes 16777232 | tf_op jit(solution)/shard_map/all_gather | solution.py:12
  658.7 1.2 while.12
  658.7 0.1 broadcast_bitcast_fusion.2
  658.8 1.0 bitcast_add_fusion.2
  659.9 0.1 copy.28
  660.1 0.3 fusion.25
  660.4 0.3 fusion.21
  660.8 138.3 %all-gather.17.cloned.1.call-done = bf16[256,4096]{0,1:T(8,128)(2,1)} async-done(((bf16[256,64]{0,1:T(8,128)(2,1)}), bf16[256,4096]{0,1:T(8,128)(2,1)}) %all-gather.17.cloned.1.call-update) | async-done | bytes 2097168 | tf_op jit(solution)/shard_map/all_gather | solution.py:125
  799.1 3.4 convolution_convert_fusion
  802.5 0.0 reduce-scatter.2.cloned.1.call-update
  802.5 37.0 %reduce-scatter.2.cloned.1.call-done = bf16[128,512]{1,0:T(8,128)(2,1)} async-done(((bf16[128,4096]{1,0:T(8,128)(2,1)}), bf16[128,512]{1,0:T(8,128)(2,1)}) %reduce-scatter.2.cloned.1.call-update) | async-done | bytes 131088 | tf_op jit(solution)/shard_map/reduce_scatter | solution.py:128
  (12 shorter events, 0.1 us)
Async XLA Ops:
  6.5 183.8 %copy-start = (bf16[128,256]{1,0:T(8,128)(2,1)S(1)}, bf16[128,256]{1,0:T(8,128)(2,1)}, u32[]{:S(2)}) copy-start(bf16[128,256]{1,0:T(8,128)(2,1)} %param.18) | copy-start | bytes 196612
  6.5 38.4 %all-gather.9.cloned.1.call-start = ((), (), s32[]{:S(2)}) async-start(), calls=%async_computation.1 | async-start | bytes 1179648 | tf_op jit(solution)/shard_map/all_gather | solution.py:32
  7.3 180.5 %all-gather.11.cloned.1.call-start = ((), (), s32[]{:S(2)}) async-start(), calls=%async_computation.2 | async-start | bytes 2129920 | tf_op jit(solution)/shard_map/all_gather | solution.py:38
  8.0 319.6 %all-gather.13.cloned.1.call-start = ((), (), s32[]{:S(2)}) async-start(), calls=%async_computation.3 | async-start | bytes 2129920 | tf_op jit(solution)/shard_map/all_gather | solution.py:39
  8.7 458.6 %all-gather.15.cloned.1.call-start = ((), (), s32[]{:S(2)}) async-start(), calls=%async_computation.4 | async-start | bytes 2129920 | tf_op jit(solution)/shard_map/all_gather | solution.py:37
  9.3 649.4 %all-gather.19.cloned.1.call-start = ((), (), s32[]{:S(2)}) async-start(), calls=%async_computation.7 | async-start | bytes 17039360 | tf_op jit(solution)/shard_map/all_gather | solution.py:12
  46.4 281.2 %copy-start.1 = (bf16[128,4096]{1,0:T(8,128)(2,1)S(1)}, bf16[128,4096]{1,0:T(8,128)(2,1)}, u32[]{:S(2)}) copy-start(bf16[128,4096]{1,0:T(8,128)(2,1)} %all-gather.9.cloned.1.call-done) | copy-start | bytes 3145732
  46.4 281.2 %copy-start.3 = (f32[4096]{0:T(1024)S(1)}, f32[4096]{0:T(1024)}, u32[]{:S(2)}) copy-start(f32[4096]{0:T(1024)} %param.13) | copy-start | bytes 49156
  190.9 140.7 %copy-start.2 = (f32[1,2]{1,0:T(1,128)S(1)}, f32[1,2]{1,0:T(1,128)}, u32[]{:S(2)}) copy-start(f32[1,2]{1,0:T(1,128)} %param.20) | copy-start | bytes 28
  190.9 213.1 %copy-start.4 = (f32[2]{0:T(128)S(1)}, f32[2]{0:T(128)}, u32[]{:S(2)}) copy-start(f32[2]{0:T(128)} %param.19) | copy-start | bytes 28
  330.9 468.2 %all-gather.17.cloned.1.call-start = ((), (), s32[]{:S(2)}) async-start(), calls=%async_computation.5 | async-start | bytes 2129920 | tf_op jit(solution)/shard_map/all_gather | solution.py:125
  331.5 508.0 %reduce-scatter.2.cloned.1.call-start = ((), (), s32[]{:S(2)}) async-start(), calls=%async_computation.6 | async-start | bytes 1179648 | tf_op jit(solution)/shard_map/reduce_scatter | solution.py:128
Sparse Core Ops, SparseCore 0:
  9.5 35.3 all-gather.8
  47.8 139.9 all-gather.10
  190.7 136.8 all-gather.12
  330.4 136.8 all-gather.14
  470.1 188.5 all-gather.18
  661.5 137.5 all-gather.16
  802.6 36.8 reduce-scatter.1
where the time goes:
time: 849 us; the launch traced here: 846 us
  waiting for transfers between devices  744 us (88%)
  blocking collectives  72.5 us (9%)
  between operations  14.3 us (2%)
  matrix products  11.3 us (1%)
    all_gather x1, waiting for transfers between devices, carried_in(): gathered = jax.tree.map(lambda a: lax.all_gather(a, axis), part)  189 us
    all_gather x1, waiting for transfers between devices, body(): lax.all_gather(w_key, 'seq', axis=0, tiled=True)  141 us
    all_gather x1, waiting for transfers between devices, body(): lax.all_gather(w_out, 'seq', axis=1, tiled=True)  138 us
    all_gather x1, waiting for transfers between devices, body(): lax.all_gather(w_value, 'seq', axis=0, tiled=True)  137 us
    all_gather x1, blocking collectives, carried_in(): gathered = jax.tree.map(lambda a: lax.all_gather(a, axis), part)  72.5 us
    all_gather x1, waiting for transfers between devices, body(): lax.all_gather(w_query, 'seq', axis=0, tiled=True)  63.3 us
    reduce_scatter x1, waiting for transfers between devices, body(): lax.psum_scatter(partial_rows.astype(jnp.bfloat16), 'head', scatter_dimen...  37 us
    all_gather x1, waiting for transfers between devices, body(): whole = lax.all_gather(tokens, 'head', axis=1, tiled=True)  34.9 us
  transfers between devices with their start and end apart: 7, of which 7 were waited for; matrix products, arithmetic and copies ran while one was open for 1% of the time, Pallas kernels for 0%

commit v1 on v0

--- a/solution.py
+++ b/solution.py
@@ -35,7 +35,9 @@
     normed = (wide * lax.rsqrt(mean_squares + 1e-05) * gain).astype(jnp.bfloat16)
     pieces = (
         lax.all_gather(w_query, "seq", axis=0, tiled=True),
-        lax.all_gather(w_key, "seq", axis=0, tiled=True),
+        jnp.concatenate(
+            lax.all_to_all(jnp.stack([w_key] * lax.axis_size("seq")), "seq", 0, 0), axis=0
+        ),
         lax.all_gather(w_value, "seq", axis=0, tiled=True),
     )
     query_sum, key_sum, value_sum = tuple(

time: 849 us -> 717 us (0.84)
  the two profiles are of different devices: /device:TPU:2 before, /device:TPU:6 now
where the time goes in v1:
time: 717 us; the launch traced here: 715 us
  waiting for transfers between devices  591 us (82%)
  blocking collectives  71.9 us (10%)
  starting transfers between devices  18.9 us (3%)
  between operations  14.3 us (2%)
  matrix products  9.61 us (1%)
    all_gather x1, waiting for transfers between devices, carried_in(): gathered = jax.tree.map(lambda a: lax.all_gather(a, axis), part)  189 us
    all_gather x1, waiting for transfers between devices, body(): lax.all_gather(w_value, 'seq', axis=0, tiled=True)  150 us
    all_gather x1, waiting for transfers between devices, body(): lax.all_gather(w_out, 'seq', axis=1, tiled=True)  137 us
    all_gather x1, blocking collectives, carried_in(): gathered = jax.tree.map(lambda a: lax.all_gather(a, axis), part)  71.9 us
    all_gather x1, waiting for transfers between devices, body(): lax.all_gather(w_query, 'seq', axis=0, tiled=True)  62.5 us
    reduce_scatter x1, waiting for transfers between devices, body(): lax.psum_scatter(partial_rows.astype(jnp.bfloat16), 'head', scatter_dimen...  37.1 us
    all_to_all x1, starting transfers between devices, body(): lax.all_to_all(jnp.stack([w_key] * lax.axis_size('seq')), 'seq', 0, 0)  18.7 us
  transfers between devices with their start and end apart: 7, of which 6 were waited for; matrix products, arithmetic and copies ran while one was open for 2% of the time, Pallas kernels for 0%

profile of v1, /device:TPU:6, one launch (start us, length us, event | category | flops | bytes accessed | tf_op | source)
XLA Modules:
  0.0 715.0 jit_solution(3076605806014958207)
XLA Ops:
  6.5 0.0 copy-start
  6.5 0.0 all-gather.8.cloned.1.call-start
  6.5 0.7 all-gather.8.cloned.1.call-update
  7.3 2.4 stack.4
  9.6 18.7 %all-to-all-start = ((bf16[64,64,256]{2,1,0:T(8,128)(2,1)}), bf16[64,64,256]{2,1,0:T(8,128)(2,1)S(1)}, u32[]{:S(2)}, u32[]{:S(2)}) async-start(bf16[64,64,256]{2,1,0:T(8,128)(2,1)} %stack.4), calls=%async_computation | async-start | bytes 4194304 | tf_op jit(solution)/shard_map/all_to_all | solution.py:39
  28.3 0.0 all-gather.10.cloned.1.call-start
  28.4 0.7 all-gather.10.cloned.1.call-update
  29.1 0.0 all-gather.12.cloned.1.call-start
  29.1 0.7 all-gather.12.cloned.1.call-update
  29.8 0.0 all-gather.16.cloned.1.call-start
  30.5 14.3 %all-gather.8.cloned.1.call-done = bf16[128,4096]{1,0:T(8,128)(2,1)} async-done(((bf16[128,512]{1,0:T(8,128)(2,1)}), bf16[128,4096]{1,0:T(8,128)(2,1)}) %all-gather.8.cloned.1.call-update) | async-done | bytes 1048592 | tf_op jit(solution)/shard_map/all_gather | solution.py:32
  44.8 1.5 fusion
  46.4 149.6 %all-gather.10.cloned.1.call-done = bf16[4096,256]{1,0:T(8,128)(2,1)} async-done(((bf16[64,256]{1,0:T(8,128)(2,1)}), bf16[4096,256]{1,0:T(8,128)(2,1)}) %all-gather.10.cloned.1.call-update) | async-done | bytes 2097168 | tf_op jit(solution)/shard_map/all_gather | solution.py:41
  196.0 2.4 convolution_convert_fusion.2
  198.4 0.1 copy.32
  198.5 0.0 all-to-all-done
  198.5 0.5 convolution_convert_fusion.3
  199.0 0.0 copy-start.2
  199.0 0.0 copy-start.4
  199.0 0.1 copy.33
  199.2 0.2 fusion.24
  199.4 0.1 fusion.52
  199.6 0.1 copy.25
  199.7 0.1 fusion.53
  199.8 0.1 copy.26
  199.9 0.7 pad_maximum_fusion
  200.6 0.0 all-gather.16.cloned.1.call-update
  200.7 0.0 all-gather.14.cloned.1.call-start
  200.7 0.5 all-gather.14.cloned.1.call-update
  201.3 0.0 reduce-scatter.2.cloned.1.call-start
  201.3 71.9 %all-gather.1 = f32[64,1,2]{2,1,0:T(1,128)S(1)} all-gather(f32[1,1,2]{2,1,0:T(1,128)S(1)} %bitcast.78), channel_id=1, replica_groups=mesh['seq'=64,'head'=8] {'seq'}, dimensions={0}, use_global_device_ids=true | all-gather | bytes 520 | tf_op jit(solution)/shard_map/all_gather | solution.py:12
  273.3 62.5 %all-gather.12.cloned.1.call-done = bf16[4096,256]{1,0:T(8,128)(2,1)} async-done(((bf16[64,256]{1,0:T(8,128)(2,1)}), bf16[4096,256]{1,0:T(8,128)(2,1)}) %all-gather.12.cloned.1.call-update) | async-done | bytes 2097168 | tf_op jit(solution)/shard_map/all_gather | solution.py:37
  335.8 2.1 fusion.26
  337.9 188.7 %all-gather.16.cloned.1.call-done = f32[128,128,256]{2,1,0:T(8,128)} async-done(((f32[2,128,256]{2,1,0:T(8,128)}), f32[128,128,256]{2,1,0:T(8,128)}) %all-gather.16.cloned.1.call-update) | async-done | bytes 16777232 | tf_op jit(solution)/shard_map/all_gather | solution.py:12
  526.6 3.5 while.12
  526.7 0.1 broadcast_bitcast_fusion.2
  526.7 1.0 bitcast_add_fusion.2
  527.8 0.1 broadcast_bitcast_fusion.2
  527.9 1.0 bitcast_add_fusion.2
  529.0 0.1 broadcast_bitcast_fusion.2
  529.1 1.0 bitcast_add_fusion.2
  530.1 0.1 copy.28
  530.3 0.3 fusion.25
  530.7 0.3 fusion.21
  531.0 136.6 %all-gather.14.cloned.1.call-done = bf16[256,4096]{0,1:T(8,128)(2,1)} async-done(((bf16[256,64]{0,1:T(8,128)(2,1)}), bf16[256,4096]{0,1:T(8,128)(2,1)}) %all-gather.14.cloned.1.call-update) | async-done | bytes 2097168 | tf_op jit(solution)/shard_map/all_gather | solution.py:127
  667.6 3.4 convolution_convert_fusion
  671.0 0.0 reduce-scatter.2.cloned.1.call-update
  671.0 37.1 %reduce-scatter.2.cloned.1.call-done = bf16[128,512]{1,0:T(8,128)(2,1)} async-done(((bf16[128,4096]{1,0:T(8,128)(2,1)}), bf16[128,512]{1,0:T(8,128)(2,1)}) %reduce-scatter.2.cloned.1.call-update) | async-done | bytes 131088 | tf_op jit(solution)/shard_map/reduce_scatter | solution.py:130
  (18 shorter events, 0.2 us)
Async XLA Ops:
  6.5 192.6 %copy-start = (bf16[128,256]{1,0:T(8,128)(2,1)S(1)}, bf16[128,256]{1,0:T(8,128)(2,1)}, u32[]{:S(2)}) copy-start(bf16[128,256]{1,0:T(8,128)(2,1)} %param.18) | copy-start | bytes 196612
  6.5 38.3 %all-gather.8.cloned.1.call-start = ((), (), s32[]{:S(2)}) async-start(), calls=%async_computation.2 | async-start | bytes 1179648 | tf_op jit(solution)/shard_map/all_gather | solution.py:32
  9.6 186.3 %copy-start.3 = (f32[4096]{0:T(1024)S(1)}, f32[4096]{0:T(1024)}, u32[]{:S(2)}) copy-start(f32[4096]{0:T(1024)} %param.13) | copy-start | bytes 49156
  9.6 188.9 %all-to-all-start = ((bf16[64,64,256]{2,1,0:T(8,128)(2,1)}), bf16[64,64,256]{2,1,0:T(8,128)(2,1)S(1)}, u32[]{:S(2)}, u32[]{:S(2)}) async-start(bf16[64,64,256]{2,1,0:T(8,128)(2,1)} %stack.4), calls=%async_computation | async-start | bytes 4194304 | tf_op jit(solution)/shard_map/all_to_all | solution.py:39
  28.3 167.6 %all-gather.10.cloned.1.call-start = ((), (), s32[]{:S(2)}) async-start(), calls=%async_computation.3 | async-start | bytes 2129920 | tf_op jit(solution)/shard_map/all_gather | solution.py:41
  29.1 306.7 %all-gather.12.cloned.1.call-start = ((), (), s32[]{:S(2)}) async-start(), calls=%async_computation.4 | async-start | bytes 2129920 | tf_op jit(solution)/shard_map/all_gather | solution.py:37
  29.8 496.8 %all-gather.16.cloned.1.call-start = ((), (), s32[]{:S(2)}) async-start(), calls=%async_computation.7 | async-start | bytes 17039360 | tf_op jit(solution)/shard_map/all_gather | solution.py:12
  46.4 152.1 %copy-start.1 = (bf16[128,4096]{1,0:T(8,128)(2,1)S(1)}, bf16[128,4096]{1,0:T(8,128)(2,1)}, u32[]{:S(2)}) copy-start(bf16[128,4096]{1,0:T(8,128)(2,1)} %all-gather.8.cloned.1.call-done) | copy-start | bytes 3145732
  199.0 2.3 copy-start.2
  199.0 74.2 %copy-start.4 = (f32[2]{0:T(128)S(1)}, f32[2]{0:T(128)}, u32[]{:S(2)}) copy-start(f32[2]{0:T(128)} %param.19) | copy-start | bytes 28
  200.7 466.9 %all-gather.14.cloned.1.call-start = ((), (), s32[]{:S(2)}) async-start(), calls=%async_computation.5 | async-start | bytes 2129920 | tf_op jit(solution)/shard_map/all_gather | solution.py:127
  201.3 506.9 %reduce-scatter.2.cloned.1.call-start = ((), (), s32[]{:S(2)}) async-start(), calls=%async_computation.6 | async-start | bytes 1179648 | tf_op jit(solution)/shard_map/reduce_scatter | solution.py:130
Sparse Core Ops, SparseCore 0:
  9.5 35.3 all-gather.7
  47.8 148.1 all-gather.9
  198.9 136.8 all-gather.11
  338.6 187.9 all-gather.15
  529.4 138.1 all-gather.13
  671.1 36.9 reduce-scatter.1
